TPU v7x, 256 devices: a whole 4x4x8 slice. The times are simulated.
256 devices in a mesh: dp: 8 (over z_lo, core), heads: 32 (over y, x, z_hi).
Axes of the slice: x: 4, y: 4, z: 8 (z_hi: 2, z_lo: 4; z = z_hi * 4 + z_lo), core: 2. Of those that a mesh axis runs over, the one named last changes fastest.
Arguments:
- latent: bfloat16 [8, 1024, 512], P(None, 'dp'), may hold values from -6 to 6
- rope_keys: bfloat16 [8, 1024, 64], P(None, 'dp'), may hold values from -6 to 6
- queries: bfloat16 [8, 1024, 24576], P(None, 'dp', 'heads'), may hold values from -320 to 320
- grad_out: bfloat16 [8, 1024, 16384], P(None, 'dp', 'heads'), may hold values from -2 to 2
- key_value_up_weight: bfloat16 [8, 512, 32768], P('dp', None, 'heads'), may hold values from -0.25 to 0.25
- momentum: bfloat16 [8, 512, 32768], P('dp', None, 'heads'), may hold values from -16 to 16
Outputs:
- new_momentum: bfloat16 [8, 512, 32768], P('dp', None, 'heads')
- layer_update_step: float32 [8, 512, 32768], P('dp', None, 'heads')
All inputs are finite; a program needn't handle non-finite values.
Results may differ from a plain program's by a relative error of at most 0.015.
Values may be sent and summed in bfloat16 or wider, within the bound.
No kernel may reach another device: no remote copies, remote signals or barrier semaphores. Data moves between devices by JAX's collectives and lax.ppermute only.
A program may use at most 64 MiB of HBM per device.

v0:
```python
import math
import jax
import jax.numpy as jnp
from jax import lax
from jax.sharding import PartitionSpec as P

LATENT = 512
HEADS = 128
NOPE = 128
ROPE = 64
VDIM = 128
STEPS = 2
poly_first = 3.4445
poly_second = -4.775
poly_third = 2.0315
norm_epsilon = 1e-07
decay_rate = 0.95


def layer_grads(compressed_latent_rows, rotary_position_rows, query_rows, grad_rows, weight_cols):
    rows = compressed_latent_rows.shape[0]
    heads_here = query_rows.shape[1] // (NOPE + ROPE)
    score_scale = 1.0 / math.sqrt(NOPE + ROPE)
    kv_rows = jnp.dot(
        compressed_latent_rows, weight_cols, preferred_element_type=jnp.float32
    ).astype(jnp.bfloat16)
    kv_rows = kv_rows.reshape(rows, heads_here, NOPE + VDIM)
    key_nope = kv_rows[:, :, :NOPE]
    values = kv_rows[:, :, NOPE:]
    query_all = query_rows.reshape(rows, heads_here, NOPE + ROPE)
    query_nope = query_all[:, :, :NOPE]
    query_rope = query_all[:, :, NOPE:]
    scores = jnp.einsum("shd,thd->hst", query_nope, key_nope, preferred_element_type=jnp.float32)
    scores = scores + jnp.einsum(
        "shd,td->hst", query_rope, rotary_position_rows, preferred_element_type=jnp.float32
    )
    scores = scores * score_scale
    places = jnp.arange(rows)
    allowed = places[None, :] <= places[:, None]
    scores = jnp.where(allowed[None], scores, -jnp.inf)
    top_score = jnp.max(scores, axis=-1, keepdims=True)
    expd = jnp.exp(scores - top_score)
    probs = expd / jnp.sum(expd, axis=-1, keepdims=True)
    probs_low = probs.astype(jnp.bfloat16)
    grad_heads = grad_rows.reshape(rows, heads_here, VDIM)
    grad_values = jnp.einsum(
        "hst,shd->thd", probs_low, grad_heads, preferred_element_type=jnp.float32
    )
    grad_probs = jnp.einsum("shd,thd->hst", grad_heads, values, preferred_element_type=jnp.float32)
    row_delta = jnp.sum(probs * grad_probs, axis=-1, keepdims=True)
    grad_scores = (probs * (grad_probs - row_delta) * score_scale).astype(jnp.bfloat16)
    grad_keys = jnp.einsum(
        "hst,shd->thd", grad_scores, query_nope, preferred_element_type=jnp.float32
    )
    joined = jnp.concatenate([grad_keys, grad_values], axis=-1).astype(jnp.bfloat16)
    return joined.reshape(rows, heads_here * (NOPE + VDIM))


def body(latent, rope_keys, queries, grad_out, key_value_up_weight, momentum):
    highest = lax.Precision.HIGHEST
    weights_all = lax.all_gather(key_value_up_weight, "dp", axis=0, tiled=True)

    def layer_body(carry, inputs):
        return (carry, layer_grads(inputs[0], inputs[1], inputs[2], inputs[3], inputs[4]))

    unused, key_value_gradient_total = lax.scan(
        layer_body, 0, (latent, rope_keys, queries, grad_out, weights_all)
    )
    grads = lax.psum_scatter(
        jnp.einsum(
            "eot,eov->etv", latent, key_value_gradient_total, preferred_element_type=jnp.float32
        ).astype(jnp.bfloat16),
        "dp",
        scatter_dimension=0,
        tiled=True,
    ).astype(jnp.float32)
    fresh = (decay_rate * momentum.astype(jnp.float32) + grads).astype(jnp.bfloat16)
    source = fresh[0].astype(jnp.float32)
    squares = lax.psum(jnp.sum(source * source), "heads")
    norm_value = jnp.sqrt(squares) + norm_epsilon
    iterate = source / norm_value
    for count_index in range(STEPS):
        gram = lax.psum(
            jnp.dot(iterate, iterate.T, precision=highest).astype(jnp.bfloat16), "heads"
        ).astype(jnp.float32)
        poly = poly_second * gram + poly_third * jnp.dot(gram, gram, precision=highest)
        iterate = poly_first * iterate + jnp.dot(poly, iterate, precision=highest)
    update_scale = 0.2 * math.sqrt(max(LATENT, HEADS * (NOPE + VDIM)))
    return (fresh, (update_scale * iterate)[None])


def solution(mesh):
    placed = (
        P(None, "dp", None),
        P(None, "dp", None),
        P(None, "dp", "heads"),
        P(None, "dp", "heads"),
        P("dp", None, "heads"),
        P("dp", None, "heads"),
    )
    return jax.shard_map(
        body,
        mesh=mesh,
        in_specs=placed,
        out_specs=(P("dp", None, "heads"), P("dp", None, "heads")),
        check_vma=False,
    )
```

profile of v0, /device:TPU:32, one launch (start us, length us, event | category | flops | bytes accessed | tf_op | source)
XLA Modules:
  0.0 1253.7 jit_solution(448452427187309342)
XLA Ops:
  7.2 0.7 all-gather.2.cloned.1.call-update
  8.0 94.5 %all-gather.2.cloned.1.call-done = bf16[8,512,1024]{2,1,0:T(8,128)(2,1)} async-done(((bf16[1,512,1024]{2,1,0:T(8,128)(2,1)}), bf16[8,512,1024]{2,1,0:T(8,128)(2,1)}) %all-gather.2.cloned.1.call-update) | async-done | bytes 8388624 | tf_op jit(solution)/shard_map/all_gather | solution.py:61
  102.4 49.9 %while.10 = (s32[]{:T(128)}, bf16[8,128,1024]{1,2,0:T(8,128)(2,1)S(1)}, bf16[8,128,768]{2,1,0:T(8,128)(2,1)}, bf16[8,128,512]{2,1,0:T(8,128)(2,1)}, bf16[8,512,1...) while((s32[]{:T(128)}, ...), condition=%wide.region_4.5_spmd, body=%wide.region_0.4_spmd.sunk | while | flops 211502464 | bytes 8906337 | solution.py:66
  102.4 0.9 constant_dynamic-slice_fusion.5
  103.5 0.9 convolution_bitcast_fusion.2
  104.5 1.6 convolution_convert_fusion.4
  106.6 0.2 fusion.99
  106.8 0.9 constant_dynamic-slice_fusion.4
  108.1 0.2 fusion.102
  108.7 0.9 constant_dynamic-slice_fusion.5
  109.8 0.9 convolution_bitcast_fusion.2
  110.7 1.6 convolution_convert_fusion.4
  112.8 0.2 fusion.99
  113.1 0.9 constant_dynamic-slice_fusion.4
  114.3 0.2 fusion.102
  114.9 0.9 constant_dynamic-slice_fusion.5
  116.0 0.9 convolution_bitcast_fusion.2
  117.0 1.6 convolution_convert_fusion.4
  119.1 0.2 fusion.99
  119.3 0.9 constant_dynamic-slice_fusion.4
  120.6 0.2 fusion.102
  121.2 0.9 constant_dynamic-slice_fusion.5
  122.3 0.9 convolution_bitcast_fusion.2
  123.2 1.6 convolution_convert_fusion.4
  125.3 0.2 fusion.99
  125.6 0.9 constant_dynamic-slice_fusion.4
  126.8 0.2 fusion.102
  127.4 0.9 constant_dynamic-slice_fusion.5
  128.5 0.9 convolution_bitcast_fusion.2
  129.4 1.6 convolution_convert_fusion.4
  131.6 0.2 fusion.99
  131.8 0.9 constant_dynamic-slice_fusion.4
  133.0 0.2 fusion.102
  133.6 0.9 constant_dynamic-slice_fusion.5
  134.7 0.9 convolution_bitcast_fusion.2
  135.7 1.6 convolution_convert_fusion.4
  138.0 0.9 constant_dynamic-slice_fusion.4
  139.3 0.2 fusion.102
  139.9 0.9 constant_dynamic-slice_fusion.5
  141.0 0.9 convolution_bitcast_fusion.2
  141.9 1.6 convolution_convert_fusion.4
  144.3 0.9 constant_dynamic-slice_fusion.4
  145.5 0.2 fusion.102
  146.1 0.9 constant_dynamic-slice_fusion.5
  147.2 0.9 convolution_bitcast_fusion.2
  148.2 1.6 convolution_convert_fusion.4
  150.5 0.9 constant_dynamic-slice_fusion.4
  151.8 0.2 fusion.102
  152.3 6.8 convert_bitcast_fusion
  159.2 1.1 copy-done
  160.3 0.5 copy.41
  160.9 91.8 %reduce-scatter.2.cloned.1.call-done = bf16[1,512,1024]{1,2,0:T(8,128)(2,1)} async-done(((bf16[8,512,1024]{1,2,0:T(8,128)(2,1)}), bf16[1,512,1024]{1,2,0:T(8,128)(2,1)}) %reduce-scatter.2.cloned.1.call-update) | async-done | bytes 1048592 | tf_op jit(solution)/shard_map/reduce_scatter | solution.py:69
  252.7 2.4 fusion.34
  255.1 119.8 %psum.21 = f32[]{:T(128)} all-reduce(f32[]{:T(128)} %get-tuple-element.74), channel_id=1, replica_groups=mesh['dp'=8,'heads'=32] {'heads'}, use_global_device_ids=true, to_apply=%region_7.8 | all-reduce | flops 1 | bytes 8 | tf_op jit(solution)/shard_map/psum | solution.py:79
  375.6 4.4 fusion.41
  380.3 419.3 %all-reduce.3.cloned.1.call-done = bf16[512,512]{1,0:T(8,128)(2,1)} async-done(((bf16[512,512]{1,0:T(8,128)(2,1)}), bf16[512,512]{1,0:T(8,128)(2,1)}) %all-reduce.3.cloned.1.call-update) | async-done | bytes 524304 | tf_op jit(solution)/shard_map/psum | solution.py:83
  799.6 1.8 fusion.40
  801.4 3.6 multiply_add_fusion
  805.0 4.3 convolution_convert_fusion.2
  809.4 1.3 copy.46
  810.7 426.9 %all-reduce.5.cloned.1.call-done = bf16[512,512]{1,0:T(8,128)(2,1)} async-done(((bf16[512,512]{1,0:T(8,128)(2,1)}), bf16[512,512]{1,0:T(8,128)(2,1)}) %all-reduce.5.cloned.1.call-update) | async-done | bytes 524304 | tf_op jit(solution)/shard_map/psum | solution.py:83
  1237.5 1.8 fusion.39
  1239.4 4.9 multiply_bitcast_fusion
  1244.3 2.9 copy.47
  (92 shorter events, 10.9 us)
Async XLA Ops:
  7.2 95.3 %all-gather.2.cloned.1.call-start = ((), (), s32[]{:S(2)}) async-start(), calls=%async_computation.1 | async-start | bytes 9437184 | tf_op jit(solution)/shard_map/all_gather | solution.py:61
  7.9 244.8 %reduce-scatter.2.cloned.1.call-start = ((), (), s32[]{:S(2)}) async-start(), calls=%async_computation.2 | async-start | bytes 9437184 | tf_op jit(solution)/shard_map/reduce_scatter | solution.py:69
  159.1 1.2 copy-start
  159.2 640.5 %all-reduce.3.cloned.1.call-start = ((), (), s32[]{:S(2)}) async-start(), calls=%async_computation.3 | async-start | bytes 1048576 | tf_op jit(solution)/shard_map/psum | solution.py:83
  380.1 857.5 %all-reduce.5.cloned.1.call-start = ((), (), s32[]{:S(2)}) async-start(), calls=%async_computation.4 | async-start | bytes 1048576 | tf_op jit(solution)/shard_map/psum | solution.py:83
Sparse Core Ops, SparseCore 0:
  9.8 92.6 all-gather.1
  159.3 93.3 reduce-scatter.1
  380.2 419.3 all-reduce.2
  809.5 428.0 all-reduce.4
where the time goes:
time: 1260 us; the launch traced here: 1250 us
  waiting for transfers between devices  1030 us (82%)
  blocking collectives  120 us (10%)
  matrix products  54.8 us (4%)
  local copies, waits for them, and re-layouts  25.5 us (2%)
  between operations  14.5 us (1%)
    psum x2, waiting for transfers between devices, body(): lax.psum(jnp.dot(iterate, iterate.T, precision=highest).astype(jnp.bfloat...  846 us
    psum x1, blocking collectives, body(): squares = lax.psum(jnp.sum(source * source), 'heads')  120 us
    all_gather x1, waiting for transfers between devices, body(): weights_all = lax.all_gather(key_value_up_weight, 'dp', axis=0, tiled=True)  94.5 us
    reduce_scatter x1, waiting for transfers between devices, body(): lax.psum_scatter(jnp.einsum('eot,eov->etv', latent, key_value_gradient_to...  91.8 us
  transfers between devices with their start and end apart: 4, of which 4 were waited for; matrix products, arithmetic and copies ran while one was open for 0% of the time, Pallas kernels for 0%

commit v1 on v0

--- a/solution.py
+++ b/solution.py
@@ -80,8 +80,11 @@
     norm_value = jnp.sqrt(squares) + norm_epsilon
     iterate = source / norm_value
     for count_index in range(STEPS):
-        gram = lax.psum(
-            jnp.dot(iterate, iterate.T, precision=highest).astype(jnp.bfloat16), "heads"
+        gram = jnp.sum(
+            lax.all_gather(
+                jnp.dot(iterate, iterate.T, precision=highest).astype(jnp.bfloat16), "heads"
+            ),
+            axis=0,
         ).astype(jnp.float32)
         poly = poly_second * gram + poly_third * jnp.dot(gram, gram, precision=highest)
         iterate = poly_first * iterate + jnp.dot(poly, iterate, precision=highest)

time: 1260 us -> 902 us (0.72)
  waiting for transfers between devices: 1030 us -> 662 us
  other arithmetic: 4.63 us -> 22.4 us
    psum x2 -> x0, waiting for transfers between devices: 846 us -> none  [body(): lax.psum(jnp.dot(iterate, iterate.T, precision=highest).astype(jnp.bfloat...]
    all_gather x0 -> x2, waiting for transfers between devices: none -> 475 us  [body(): lax.all_gather(jnp.dot(iterate, iterate.T, precision=highest).astype(jnp....]
    reduce_sum x0 -> x2, other arithmetic: none -> 17.8 us  [body(): jnp.sum(lax.all_gather(jnp.dot(iterate, iterate.T, precision=highest).ast...]
where the time goes in v1:
time: 902 us; the launch traced here: 898 us
  waiting for transfers between devices  662 us (73%)
  blocking collectives  120 us (13%)
  matrix products  52 us (6%)
  local copies, waits for them, and re-layouts  25.5 us (3%)
  other arithmetic  22.4 us (2%)
  between operations  14.5 us (2%)
    all_gather x2, waiting for transfers between devices, body(): lax.all_gather(jnp.dot(iterate, iterate.T, precision=highest).astype(jnp....  475 us
    psum x1, blocking collectives, body(): squares = lax.psum(jnp.sum(source * source), 'heads')  120 us
    all_gather x1, waiting for transfers between devices, body(): weights_all = lax.all_gather(key_value_up_weight, 'dp', axis=0, tiled=True)  94.5 us
    reduce_scatter x1, waiting for transfers between devices, body(): lax.psum_scatter(jnp.einsum('eot,eov->etv', latent, key_value_gradient_to...  91.8 us
  transfers between devices with their start and end apart: 4, of which 4 were waited for; matrix products, arithmetic and copies ran while one was open for 0% of the time, Pallas kernels for 0%

profile of v1, /device:TPU:32, one launch (start us, length us, event | category | flops | bytes accessed | tf_op | source)
XLA Modules:
  0.0 898.0 jit_solution(16573973369363047029)
XLA Ops:
  7.2 0.7 all-gather.6.cloned.1.call-update
  8.0 94.5 %all-gather.6.cloned.1.call-done = bf16[8,512,1024]{2,1,0:T(8,128)(2,1)} async-done(((bf16[1,512,1024]{2,1,0:T(8,128)(2,1)}), bf16[8,512,1024]{2,1,0:T(8,128)(2,1)}) %all-gather.6.cloned.1.call-update) | async-done | bytes 8388624 | tf_op jit(solution)/shard_map/all_gather | solution.py:61
  102.4 50.0 %while.10 = (s32[]{:T(128)}, bf16[8,128,1024]{1,2,0:T(8,128)(2,1)S(1)}, bf16[8,128,768]{2,1,0:T(8,128)(2,1)}, bf16[8,128,512]{2,1,0:T(8,128)(2,1)}, bf16[8,512,1...) while((s32[]{:T(128)}, ...), condition=%wide.region_4.5_spmd, body=%wide.region_0.4_spmd.sunk | while | flops 211502464 | bytes 8905837 | solution.py:66
  102.5 0.9 constant_dynamic-slice_fusion.4
  103.5 0.9 constant_dynamic-slice_fusion.5
  104.6 0.9 convolution_bitcast_fusion.2
  105.5 1.6 convolution_convert_fusion.4
  107.8 0.2 fusion.99
  108.3 0.2 fusion.102
  108.7 0.9 constant_dynamic-slice_fusion.4
  109.7 0.9 constant_dynamic-slice_fusion.5
  110.9 0.9 convolution_bitcast_fusion.2
  111.8 1.6 convolution_convert_fusion.4
  114.1 0.2 fusion.99
  114.6 0.2 fusion.102
  114.9 0.9 constant_dynamic-slice_fusion.4
  116.0 0.9 constant_dynamic-slice_fusion.5
  117.1 0.9 convolution_bitcast_fusion.2
  118.0 1.6 convolution_convert_fusion.4
  120.3 0.2 fusion.99
  120.8 0.2 fusion.102
  121.2 0.9 constant_dynamic-slice_fusion.4
  122.2 0.9 constant_dynamic-slice_fusion.5
  123.4 0.9 convolution_bitcast_fusion.2
  124.3 1.6 convolution_convert_fusion.4
  127.1 0.2 fusion.102
  127.4 0.9 constant_dynamic-slice_fusion.4
  128.5 0.9 constant_dynamic-slice_fusion.5
  129.6 0.9 convolution_bitcast_fusion.2
  130.5 1.6 convolution_convert_fusion.4
  133.3 0.2 fusion.102
  133.7 0.9 constant_dynamic-slice_fusion.4
  134.7 0.9 constant_dynamic-slice_fusion.5
  135.9 0.9 convolution_bitcast_fusion.2
  136.8 1.6 convolution_convert_fusion.4
  139.6 0.2 fusion.102
  139.9 0.9 constant_dynamic-slice_fusion.4
  141.0 0.9 constant_dynamic-slice_fusion.5
  142.1 0.9 convolution_bitcast_fusion.2
  143.0 1.6 convolution_convert_fusion.4
  145.8 0.2 fusion.102
  146.2 0.9 constant_dynamic-slice_fusion.4
  147.2 0.9 constant_dynamic-slice_fusion.5
  148.3 0.9 convolution_bitcast_fusion.2
  149.3 1.6 convolution_convert_fusion.4
  152.1 0.2 fusion.102
  152.4 6.8 convert_bitcast_fusion
  159.3 1.1 copy-done
  160.4 0.5 copy.41
  160.9 91.8 %reduce-scatter.2.cloned.1.call-done = bf16[1,512,1024]{1,2,0:T(8,128)(2,1)} async-done(((bf16[8,512,1024]{1,2,0:T(8,128)(2,1)}), bf16[1,512,1024]{1,2,0:T(8,128)(2,1)}) %reduce-scatter.2.cloned.1.call-update) | async-done | bytes 1048592 | tf_op jit(solution)/shard_map/reduce_scatter | solution.py:69
  252.8 2.4 fusion.34
  255.1 119.8 %psum.7 = f32[]{:T(128)} all-reduce(f32[]{:T(128)} %get-tuple-element.74), channel_id=1, replica_groups=mesh['dp'=8,'heads'=32] {'heads'}, use_global_device_ids=true, to_apply=%region_7.8 | all-reduce | flops 1 | bytes 8 | tf_op jit(solution)/shard_map/psum | solution.py:79
  375.6 4.4 fusion.41
  380.4 236.0 %all-gather.8.cloned.1.call-done = bf16[16384,512]{1,0:T(8,128)(2,1)} async-done(((bf16[512,512]{1,0:T(8,128)(2,1)}), bf16[16384,512]{1,0:T(8,128)(2,1)}) %all-gather.8.cloned.1.call-update) | async-done | bytes 16777232 | tf_op jit(solution)/shard_map/all_gather | solution.py:84
  616.3 8.8 reduce_sum.52
  625.1 0.4 fusion.40
  625.6 3.6 multiply_add_fusion
  629.2 4.3 convolution_convert_fusion.2
  633.5 1.3 copy.46
  634.8 239.3 %all-gather.10.cloned.1.call-done = bf16[16384,512]{1,0:T(8,128)(2,1)} async-done(((bf16[512,512]{1,0:T(8,128)(2,1)}), bf16[16384,512]{1,0:T(8,128)(2,1)}) %all-gather.10.cloned.1.call-update) | async-done | bytes 16777232 | tf_op jit(solution)/shard_map/all_gather | solution.py:84
  874.2 9.0 %reduce_sum.53 = bf16[512,512]{1,0:T(8,128)(2,1)S(1)} reduce(bf16[32,512,512]{2,1,0:T(8,128)(2,1)} %bitcast.79, bf16[]{:T(256)} %constant.17.clone.1), dimensions={0}, to_apply=%region_9.10 | reduce | flops 8126464 | bytes 17301506 | tf_op jit(solution)/shard_map/reduce_sum | solution.py:83
  883.2 0.4 fusion.39
  883.6 4.9 multiply_bitcast_fusion
  888.5 2.9 copy.47
  (94 shorter events, 11.4 us)
Async XLA Ops:
  7.2 95.3 %all-gather.6.cloned.1.call-start = ((), (), s32[]{:S(2)}) async-start(), calls=%async_computation.1 | async-start | bytes 9437184 | tf_op jit(solution)/shard_map/all_gather | solution.py:61
  7.9 244.9 %reduce-scatter.2.cloned.1.call-start = ((), (), s32[]{:S(2)}) async-start(), calls=%async_computation.2 | async-start | bytes 9437184 | tf_op jit(solution)/shard_map/reduce_scatter | solution.py:69
  159.2 1.2 copy-start
  159.2 457.1 %all-gather.8.cloned.1.call-start = ((), (), s32[]{:S(2)}) async-start(), calls=%async_computation.3 | async-start | bytes 17301504 | tf_op jit(solution)/shard_map/all_gather | solution.py:84
  380.1 494.0 %all-gather.10.cloned.1.call-start = ((), (), s32[]{:S(2)}) async-start(), calls=%async_computation.4 | async-start | bytes 17301504 | tf_op jit(solution)/shard_map/all_gather | solution.py:84
Sparse Core Ops, SparseCore 0:
  9.8 92.6 all-gather.5
  159.3 93.3 reduce-scatter.1
  380.2 236.0 all-gather.7
  633.6 240.4 all-gather.9

commit v2 on v0

--- a/solution.py
+++ b/solution.py
@@ -58,7 +58,9 @@
 
 def body(latent, rope_keys, queries, grad_out, key_value_up_weight, momentum):
     highest = lax.Precision.HIGHEST
-    weights_all = lax.all_gather(key_value_up_weight, "dp", axis=0, tiled=True)
+    weights_all = jnp.concatenate(
+        lax.all_to_all(jnp.stack([key_value_up_weight] * lax.axis_size("dp")), "dp", 0, 0), axis=0
+    )
 
     def layer_body(carry, inputs):
         return (carry, layer_grads(inputs[0], inputs[1], inputs[2], inputs[3], inputs[4]))

time: 1260 us -> 1360 us (1.079)
  waiting for transfers between devices: 1030 us -> 1120 us
    all_to_all x0 -> x1, waiting for transfers between devices: none -> 180 us  [body(): lax.all_to_all(jnp.stack([key_value_up_weight] * lax.axis_size('dp')), 'd...]
    all_gather x1 -> x0, waiting for transfers between devices: 94.5 us -> none  [body(): weights_all = lax.all_gather(key_value_up_weight, 'dp', axis=0, tiled=True)]
where the time goes in v2:
time: 1360 us
  waiting for transfers between devices  1120 us (82%)
  blocking collectives  120 us (9%)
  matrix products  54.5 us (4%)
  local copies, waits for them, and re-layouts  36.5 us (3%)
  between operations  14.5 us (1%)
    psum x2, waiting for transfers between devices, body(): lax.psum(jnp.dot(iterate, iterate.T, precision=highest).astype(jnp.bfloat...  846 us
    all_to_all x1, waiting for transfers between devices, body(): lax.all_to_all(jnp.stack([key_value_up_weight] * lax.axis_size('dp')), 'd...  180 us
    psum x1, blocking collectives, body(): squares = lax.psum(jnp.sum(source * source), 'heads')  120 us
    reduce_scatter x1, waiting for transfers between devices, body(): lax.psum_scatter(jnp.einsum('eot,eov->etv', latent, key_value_gradient_to...  93.8 us
  transfers between devices with their start and end apart: 4, of which 4 were waited for; matrix products, arithmetic and copies ran while one was open for 0% of the time, Pallas kernels for 0%

profile of v2, /device:TPU:32, one launch (start us, length us, event | category | flops | bytes accessed | tf_op | source)
XLA Modules:
  0.0 1358.1 jit_solution(15985667567111436438)
XLA Ops:
  7.2 5.5 stack.2
  12.7 6.8 all-to-all-start
  19.5 180.4 %all-to-all-done = bf16[8,1,512,1024]{3,2,1,0:T(8,128)(2,1)} async-done(((bf16[8,1,512,1024]{3,2,1,0:T(8,128)(2,1)}), bf16[8,1,512,1024]{3,2,1,0:T(8,128)(2,1)}, u32[]{:S(2)}, u32[]{:S(2)}) %all-to-all-start) | async-done | bytes 8388640 | tf_op jit(solution)/shard_map/all_to_all | solution.py:62
  199.9 54.6 %while.10 = (s32[]{:T(128)}, bf16[8,128,1024]{1,2,0:T(8,128)(2,1)}, bf16[8,128,768]{2,1,0:T(8,128)(2,1)}, bf16[8,128,512]{2,1,0:T(8,128)(2,1)S(1)}, bf16[8,512,1...) while((s32[]{:T(128)}, bf16[8,128,1024]{1,2,0:T(8,128)(2,1)}, ...), condition=%wide.region_4.5_spmd, body=%wide.region_0.4_spmd.sunk | while | flops 211502464 | bytes 8906845 | solution.py:68
  199.9 0.9 constant_dynamic-slice_fusion.5
  201.0 0.9 convolution_bitcast_fusion.2
  201.9 1.5 convolution_convert_fusion.4
  204.2 0.9 constant_dynamic-slice_fusion.4
  205.5 0.2 fusion.102
  206.0 0.7 constant_dynamic-update-slice_fusion.2
  206.7 0.9 constant_dynamic-slice_fusion.5
  207.8 0.9 convolution_bitcast_fusion.2
  208.8 1.5 convolution_convert_fusion.4
  211.1 0.9 constant_dynamic-slice_fusion.4
  212.8 0.7 constant_dynamic-update-slice_fusion.2
  213.5 0.9 constant_dynamic-slice_fusion.5
  214.6 0.9 convolution_bitcast_fusion.2
  215.6 1.5 convolution_convert_fusion.4
  217.9 0.9 constant_dynamic-slice_fusion.4
  219.1 0.2 fusion.102
  219.6 0.7 constant_dynamic-update-slice_fusion.2
  220.4 0.9 constant_dynamic-slice_fusion.5
  221.5 0.9 convolution_bitcast_fusion.2
  222.4 1.5 convolution_convert_fusion.4
  224.7 0.9 constant_dynamic-slice_fusion.4
  226.5 0.7 constant_dynamic-update-slice_fusion.2
  227.2 0.9 constant_dynamic-slice_fusion.5
  228.3 0.9 convolution_bitcast_fusion.2
  229.2 1.5 convolution_convert_fusion.4
  231.5 0.9 constant_dynamic-slice_fusion.4
  233.3 0.7 constant_dynamic-update-slice_fusion.2
  234.0 0.9 constant_dynamic-slice_fusion.5
  235.1 0.9 convolution_bitcast_fusion.2
  236.0 1.5 convolution_convert_fusion.4
  238.3 0.9 constant_dynamic-slice_fusion.4
  239.6 0.2 fusion.102
  240.1 0.7 constant_dynamic-update-slice_fusion.2
  240.8 0.9 constant_dynamic-slice_fusion.5
  241.9 0.9 convolution_bitcast_fusion.2
  242.9 1.5 convolution_convert_fusion.4
  245.2 0.9 constant_dynamic-slice_fusion.4
  246.9 0.7 constant_dynamic-update-slice_fusion.2
  247.6 0.9 constant_dynamic-slice_fusion.5
  248.7 0.9 convolution_bitcast_fusion.2
  249.7 1.5 convolution_convert_fusion.4
  252.0 0.9 constant_dynamic-slice_fusion.4
  253.2 0.2 fusion.102
  253.7 0.7 constant_dynamic-update-slice_fusion.2
  254.5 7.1 convert_bitcast_fusion
  261.7 1.1 copy-done.1
  262.8 0.5 copy.41
  263.4 93.8 %reduce-scatter.2.cloned.1.call-done = bf16[1,512,1024]{1,2,0:T(8,128)(2,1)} async-done(((bf16[8,512,1024]{1,2,0:T(8,128)(2,1)}), bf16[1,512,1024]{1,2,0:T(8,128)(2,1)}) %reduce-scatter.2.cloned.1.call-update) | async-done | bytes 1048592 | tf_op jit(solution)/shard_map/reduce_scatter | solution.py:71
  357.1 2.4 fusion.34
  359.5 119.8 %psum.21 = f32[]{:T(128)} all-reduce(f32[]{:T(128)} %get-tuple-element.74), channel_id=1, replica_groups=mesh['dp'=8,'heads'=32] {'heads'}, use_global_device_ids=true, to_apply=%region_7.8 | all-reduce | flops 1 | bytes 8 | tf_op jit(solution)/shard_map/psum | solution.py:81
  480.0 4.4 fusion.41
  484.7 419.4 %all-reduce.3.cloned.1.call-done = bf16[512,512]{1,0:T(8,128)(2,1)} async-done(((bf16[512,512]{1,0:T(8,128)(2,1)}), bf16[512,512]{1,0:T(8,128)(2,1)}) %all-reduce.3.cloned.1.call-update) | async-done | bytes 524304 | tf_op jit(solution)/shard_map/psum | solution.py:85
  904.1 1.8 fusion.40
  906.0 3.6 multiply_add_fusion
  909.5 4.3 convolution_convert_fusion.2
  913.9 1.3 copy.46
  915.2 426.8 %all-reduce.5.cloned.1.call-done = bf16[512,512]{1,0:T(8,128)(2,1)} async-done(((bf16[512,512]{1,0:T(8,128)(2,1)}), bf16[512,512]{1,0:T(8,128)(2,1)}) %all-reduce.5.cloned.1.call-update) | async-done | bytes 524304 | tf_op jit(solution)/shard_map/psum | solution.py:85
  1342.0 1.8 fusion.39
  1343.8 4.9 multiply_bitcast_fusion
  1348.7 2.9 copy.47
  (94 shorter events, 12.8 us)
Async XLA Ops:
  12.7 187.2 %copy-start = (bf16[8,128,512]{2,1,0:T(8,128)(2,1)S(1)}, bf16[8,128,512]{2,1,0:T(8,128)(2,1)}, u32[]{:S(2)}) copy-start(bf16[8,128,512]{2,1,0:T(8,128)(2,1)} %param.8) | copy-start | bytes 3145732
  12.7 187.2 %all-to-all-start = ((bf16[8,1,512,1024]{3,2,1,0:T(8,128)(2,1)}), bf16[8,1,512,1024]{3,2,1,0:T(8,128)(2,1)}, u32[]{:S(2)}, u32[]{:S(2)}) async-start(bf16[8,1,512,1024]{3,2,1,0:T(8,128)(2,1)} %stack.2), calls=%async_computation | async-start | bytes 16777216 | tf_op jit(solution)/shard_map/all_to_all | solution.py:62
  19.5 337.7 %reduce-scatter.2.cloned.1.call-start = ((), (), s32[]{:S(2)}) async-start(), calls=%async_computation.2 | async-start | bytes 9437184 | tf_op jit(solution)/shard_map/reduce_scatter | solution.py:71
  261.6 1.2 copy-start.1
  261.6 642.5 %all-reduce.3.cloned.1.call-start = ((), (), s32[]{:S(2)}) async-start(), calls=%async_computation.3 | async-start | bytes 1048576 | tf_op jit(solution)/shard_map/psum | solution.py:85
  484.5 857.4 %all-reduce.5.cloned.1.call-start = ((), (), s32[]{:S(2)}) async-start(), calls=%async_computation.4 | async-start | bytes 1048576 | tf_op jit(solution)/shard_map/psum | solution.py:85
Sparse Core Ops, SparseCore 0:
  261.8 95.3 reduce-scatter.1
  484.6 419.4 all-reduce.2
  914.0 427.9 all-reduce.4
